TPU v7x, 256 devices: a whole 4x4x8 slice. The times are simulated.
256 devices in a mesh: node: 32 (over z, y), head: 8 (over x, core).
Axes of the slice: x: 4, y: 4, z: 8, core: 2. Of those that a mesh axis runs over, the one named last changes fastest.
Arguments:
- query_rows: bfloat16 [32768, 1024], P(('node', 'head')), may hold values from -6 to 6
- key_rows: bfloat16 [32768, 1024], P(('node', 'head')), may hold values from -6 to 6
- value_rows: bfloat16 [32768, 1024], P(('node', 'head')), may hold values from -6 to 6
- grad_out: bfloat16 [32768, 1024], P(('node', 'head')), may hold values from -6 to 6
- heat_bias: bfloat16 [256, 16, 128, 128], P('node'), may hold values from -5 to 5
- block_pattern: int32 [256, 16], P('node'), may hold values from -1 to 255, as said below
Outputs:
- grad_query: bfloat16 [32768, 1024], P(('node', 'head'))
- grad_key: bfloat16 [32768, 1024], P(('node', 'head'))
- grad_value: bfloat16 [32768, 1024], P(('node', 'head'))
Inputs may be any that keep to these rules, and one draw needn't show every extreme that they name: `block_pattern`: entry (c, j) names a key cluster of query cluster c or is -1 for an empty slot; slot 0 names c itself, and every named cluster c2 has c2 // 8 within 2 of c // 8.
All inputs are finite; a program needn't handle non-finite values.
Results may differ from a plain program's by a relative error of at most 0.011.
Values may be sent and summed in bfloat16 or wider, within the bound.
A program may use at most 128 MiB of HBM per device.

v0:
```python
import jax
import jax.numpy as jnp
from jax import lax
from jax.sharding import PartitionSpec as P

CL = 128
HDIM = 64
NB = 16
REACH = 2


def shifted(array, axis, by):
    size = lax.axis_size(axis)
    pairs = [(i, i + by) for i in range(size) if 0 <= i + by < size]
    return lax.ppermute(array, axis, pairs)


def as_sent(array):
    return jax.tree.map(lambda a: a.astype(jnp.bfloat16) if a.dtype == jnp.float32 else a, array)


def on_device(query_rows, key_rows, value_rows, grad_out, heat_bias, block_pattern):
    local_q, local_k, local_v, local_g = (
        lax.all_to_all(query_rows, "head", split_axis=1, concat_axis=0, tiled=True),
        lax.all_to_all(key_rows, "head", split_axis=1, concat_axis=0, tiled=True),
        lax.all_to_all(value_rows, "head", split_axis=1, concat_axis=0, tiled=True),
        lax.all_to_all(grad_out, "head", split_axis=1, concat_axis=0, tiled=True),
    )
    rows, width = local_q.shape
    count = rows // CL
    heads_here = width // HDIM
    shard = lax.axis_index("node")
    scale = HDIM ** (-0.5)
    fetched = {0: (local_k, local_v)}
    for offset in range(-REACH, REACH + 1):
        if offset != 0:
            fetched[offset] = shifted((local_k, local_v), "node", -offset)
    span = 2 * REACH + 1
    offsets = list(range(-REACH, REACH + 1))
    near_count = span * count
    flat_shape = (near_count, CL * width)
    near_keys = jnp.concatenate([fetched[o][0] for o in offsets], axis=0).reshape(flat_shape)
    near_values = jnp.concatenate([fetched[o][1] for o in offsets], axis=0).reshape(flat_shape)
    valid = block_pattern >= 0
    local_index = jnp.where(valid, block_pattern - (shard - REACH) * count, 0)
    group = min(4, count)
    turns = count // group
    q_groups = local_q.reshape(turns, group, CL, width)
    g_groups = local_g.reshape(turns, group, CL, width)
    b_groups = heat_bias.reshape(turns, group, NB, CL, CL)
    i_groups = local_index.reshape(turns, group, NB)
    v_groups = valid.reshape(turns, group, NB)

    def advance(carry, inputs):
        grad_k, grad_v = carry
        q_blk, g_blk, b_blk, index, present = inputs
        targets = lax.broadcasted_iota(jnp.int32, (group * NB, near_count), 1)
        picks = index.reshape(-1)[:, None] == targets
        pick_half = picks.astype(jnp.bfloat16)
        live = (picks & present.reshape(-1)[:, None]).astype(jnp.float32)
        k_blk = (
            jnp.dot(pick_half, near_keys, preferred_element_type=jnp.float32)
            .astype(jnp.bfloat16)
            .reshape(group, NB, CL, width)
        )
        v_blk = (
            jnp.dot(pick_half, near_values, preferred_element_type=jnp.float32)
            .astype(jnp.bfloat16)
            .reshape(group, NB, CL, width)
        )
        bias = b_blk.astype(jnp.float32)
        mask = present[:, :, None, None]
        grad_q_heads = []
        part_k_heads = []
        part_v_heads = []
        for head in range(heads_here):
            lo = head * HDIM
            hi = lo + HDIM
            q_head = q_blk[:, :, lo:hi]
            g_head = g_blk[:, :, lo:hi]
            k_head = k_blk[:, :, :, lo:hi]
            v_head = v_blk[:, :, :, lo:hi]
            scores = (
                jnp.einsum("brd,bjcd->bjrc", q_head, k_head, preferred_element_type=jnp.float32)
                * scale
                + bias
            )
            scores = jnp.where(mask, scores, -jnp.inf)
            top = jnp.max(scores, axis=(1, 3), keepdims=True)
            prob = jnp.exp(scores - top)
            prob = prob / jnp.sum(prob, axis=(1, 3), keepdims=True)
            prob_half = prob.astype(jnp.bfloat16)
            attended = jnp.einsum(
                "bjrc,bjcd->brd", prob_half, v_head, preferred_element_type=jnp.float32
            )
            delta = jnp.sum(g_head.astype(jnp.float32) * attended, axis=2)
            dprob = jnp.einsum("brd,bjcd->bjrc", g_head, v_head, preferred_element_type=jnp.float32)
            dscore = prob * (dprob - delta[:, None, :, None])
            dscore_half = dscore.astype(jnp.bfloat16)
            grad_q_heads.append(
                jnp.einsum(
                    "bjrc,bjcd->brd", dscore_half, k_head, preferred_element_type=jnp.float32
                )
                * scale
            )
            part_k_heads.append(
                jnp.einsum(
                    "bjrc,brd->bjcd", dscore_half, q_head, preferred_element_type=jnp.float32
                )
                * scale
            )
            part_v_heads.append(
                jnp.einsum("bjrc,brd->bjcd", prob_half, g_head, preferred_element_type=jnp.float32)
            )
        grad_q = jnp.concatenate(grad_q_heads, axis=-1)
        part_k = jnp.concatenate(part_k_heads, axis=-1).reshape(group * NB, CL * width)
        part_v = jnp.concatenate(part_v_heads, axis=-1).reshape(group * NB, CL * width)
        grad_k = grad_k + jnp.dot(
            live.T, part_k, precision=lax.Precision.HIGHEST, preferred_element_type=jnp.float32
        )
        grad_v = grad_v + jnp.dot(
            live.T, part_v, precision=lax.Precision.HIGHEST, preferred_element_type=jnp.float32
        )
        return ((grad_k, grad_v), grad_q)

    start = (jnp.zeros(flat_shape, jnp.float32), jnp.zeros(flat_shape, jnp.float32))
    (grad_k, grad_v), grad_q = lax.scan(
        advance, start, (q_groups, g_groups, b_groups, i_groups, v_groups)
    )

    def partial_pair(offset):
        first = (offset + REACH) * count
        return (
            grad_k[first : first + count].reshape(rows, width),
            grad_v[first : first + count].reshape(rows, width),
        )

    total_k, total_v = partial_pair(0)
    for offset in offsets:
        if offset != 0:
            arrived = shifted(as_sent(partial_pair(offset)), "node", offset)
            total_k = total_k + arrived[0]
            total_v = total_v + arrived[1]
    grad_query = grad_q.reshape(rows, width).astype(jnp.bfloat16)
    grad_key = total_k.astype(jnp.bfloat16)
    grad_value = total_v.astype(jnp.bfloat16)
    return (
        lax.all_to_all(grad_query, "head", split_axis=0, concat_axis=1, tiled=True),
        lax.all_to_all(grad_key, "head", split_axis=0, concat_axis=1, tiled=True),
        lax.all_to_all(grad_value, "head", split_axis=0, concat_axis=1, tiled=True),
    )


def solution(mesh):
    return jax.shard_map(
        on_device,
        mesh=mesh,
        in_specs=(
            P(("node", "head"), None),
            P(("node", "head"), None),
            P(("node", "head"), None),
            P(("node", "head"), None),
            P("node", None, None, None),
            P("node", None),
        ),
        out_specs=(P(("node", "head"), None), P(("node", "head"), None), P(("node", "head"), None)),
        check_vma=False,
    )
```

profile of v0, /device:TPU:1, one launch (start us, length us, event | category | flops | bytes accessed | tf_op | source)
XLA Modules:
  0.0 272.0 jit_solution(12997663211717043957)
XLA Ops:
  2.6 6.6 %all-to-all-start = ((bf16[128,8,128]{2,0,1:T(8,128)(2,1)}), bf16[128,8,128]{2,0,1:T(8,128)(2,1)S(1)}, u32[]{:S(2)}, u32[]{:S(2)}) async-start(bf16[128,8,128]{2,0,1:T(8,128)(2,1)} %copy.108), calls=%async_computation | async-start | bytes 524288 | tf_op jit(solution)/shard_map/all_to_all | solution.py:25
  11.2 4.5 %all-to-all-done = bf16[128,8,128]{2,0,1:T(8,128)(2,1)S(1)} async-done(((bf16[128,8,128]{2,0,1:T(8,128)(2,1)}), bf16[128,8,128]{2,0,1:T(8,128)(2,1)S(1)}, u32[]{:S(2)}, u32[]{:S(2)}) %all-to-all-start) | async-done | bytes 262176 | tf_op jit(solution)/shard_map/all_to_all | solution.py:25
  24.2 6.5 %copy.110 = bf16[8,16,128,128]{2,3,1,0:T(8,128)(2,1)} copy(bf16[8,16,128,128]{3,2,1,0:T(8,128)(2,1)} %param.12) | data formatting | bytes 8388608 | tf_op args[4]
  37.3 5.4 %all-to-all-start.3 = ((bf16[128,8,128]{0,2,1:T(8,128)(2,1)}), bf16[128,8,128]{0,2,1:T(8,128)(2,1)S(1)}, u32[]{:S(2)}, u32[]{:S(2)}) async-start(bf16[128,8,128]{0,2,1:T(8,128)(2,1)} %bitcast.14), calls=%async_computation.3 | async-start | bytes 524288 | tf_op jit(solution)/shard_map/all_to_all | solution.py:27
  42.7 6.1 %collective-permute-start.4 = (bf16[1024,128]{1,0:T(8,128)(2,1)S(1)}, bf16[1024,128]{1,0:T(8,128)(2,1)S(1)}, u32[]{:S(2)}, u32[]{:S(2)}) collective-permute-start(bf16[1024,128]{1,0:T(8,128)(2,1)S(1)} %bitcast.220), channel_id=1, source_target_pairs={{0,16},{8,24},{16,32},{24,40},{32,48},{40,56},{48,64},{56,72},{64,... | collective-permute-start | bytes 786440 | tf_op jit(solution)/shard_map/ppermute | solution.py:15
  54.2 5.2 %collective-permute-done.4 = bf16[1024,128]{1,0:T(8,128)(2,1)S(1)} collective-permute-done((bf16[1024,128]{1,0:T(8,128)(2,1)S(1)}, bf16[1024,128]{1,0:T(8,128)(2,1)S(1)}, u32[]{:S(2)}, u32[]{:S(2)}) %collective-permute-start.4) | collective-permute-done | bytes 262176 | tf_op jit(solution)/shard_map/ppermute | solution.py:15
  66.8 4.9 %all-to-all-start.1 = ((bf16[128,8,128]{0,2,1:T(8,128)(2,1)}), bf16[128,8,128]{0,2,1:T(8,128)(2,1)S(1)}, u32[]{:S(2)}, u32[]{:S(2)}) async-start(bf16[128,8,128]{0,2,1:T(8,128)(2,1)} %bitcast.230), calls=%async_computation.1 | async-start | bytes 524288 | tf_op jit(solution)/shard_map/all_to_all | solution.py:24
  78.1 116.1 %while.15 = (s32[]{:T(128)}, f32[40,16384]{1,0:T(8,128)}, f32[40,16384]{1,0:T(8,128)}, bf16[2,4,128,128]{2,3,1,0:T(8,128)(2,1)}, s32[2,4,16]{2,1,0:T(4,128)S(1)}...) while((s32[]{:T(128)}, f32[40,16384]{1,0:T(8,128)}, ...), condition=%wide.region_7.8_spmd.clone, body=%wide.region_0.7_spmd.clone.sunk | while | flops 2824941568 | bytes 211853616 | solution.py:127
  102.6 5.4 %copy.166 = f32[4,16,128,128]{3,2,1,0:T(8,128)} copy(f32[4,16,128,128]{2,3,1,0:T(8,128)} %pad_maximum_fusion.5) | data formatting | bytes 8388608 | tf_op jit(solution)/shard_map/while/body/eval_jaxpr/concatenate | solution.py:117
  108.1 7.9 %convolution_add_fusion.5 = f32[40,16384]{1,0:T(8,128)} fusion(f32[8,8,128,128]{3,2,1,0:T(8,128)} %bitcast.215, f32[40,16384]{1,0:T(8,128)} %get-tuple-element.240, pred[]{:T(512)S(6)} %compare.3, s32[64]{0:T(128)S(1)} %eq.53, pred[64]{0:T(512)(128)(4,1)S(1)} %and.34), kind=kOutput, calls=%fused_computation.2.clone.1 | convolution fusion | flops 504632320 | bytes 9437505 | tf_op jit(solution)/shard_map/while/body/eval_jaxpr/dot_general | solution.py:121
  121.0 5.5 %copy.165 = f32[4,16,128,128]{3,2,1,0:T(8,128)} copy(f32[4,16,128,128]{2,3,1,0:T(8,128)} %pad_maximum_fusion.4) | data formatting | bytes 8388608 | tf_op jit(solution)/shard_map/while/body/eval_jaxpr/concatenate | solution.py:116
  126.5 7.8 %convolution_add_fusion.4 = f32[40,16384]{1,0:T(8,128)S(1)} fusion(f32[8,8,128,128]{3,2,1,0:T(8,128)} %bitcast.216, f32[40,16384]{1,0:T(8,128)S(1)} %copy-done.2, pred[]{:T(512)S(6)} %compare.3, s32[64]{0:T(128)S(1)} %eq.53, pred[64]{0:T(512)(128)(4,1)S(1)} %and.34), kind=kOutput, calls=%fused_computation.3.clone.1 | convolution fusion | flops 504632320 | bytes 9437505 | tf_op jit(solution)/shard_map/while/body/eval_jaxpr/dot_general | solution.py:118
  160.3 5.4 %copy.166 = f32[4,16,128,128]{3,2,1,0:T(8,128)} copy(f32[4,16,128,128]{2,3,1,0:T(8,128)} %pad_maximum_fusion.5) | data formatting | bytes 8388608 | tf_op jit(solution)/shard_map/while/body/eval_jaxpr/concatenate | solution.py:117
  165.8 8.7 %convolution_add_fusion.5 = f32[40,16384]{1,0:T(8,128)} fusion(f32[8,8,128,128]{3,2,1,0:T(8,128)} %bitcast.215, f32[40,16384]{1,0:T(8,128)} %get-tuple-element.240, pred[]{:T(512)S(6)} %compare.3, s32[64]{0:T(128)S(1)} %eq.53, pred[64]{0:T(512)(128)(4,1)S(1)} %and.34), kind=kOutput, calls=%fused_computation.2.clone.1 | convolution fusion | flops 504632320 | bytes 9437505 | tf_op jit(solution)/shard_map/while/body/eval_jaxpr/dot_general | solution.py:121
  179.4 5.5 %copy.165 = f32[4,16,128,128]{3,2,1,0:T(8,128)} copy(f32[4,16,128,128]{2,3,1,0:T(8,128)} %pad_maximum_fusion.4) | data formatting | bytes 8388608 | tf_op jit(solution)/shard_map/while/body/eval_jaxpr/concatenate | solution.py:116
  185.0 7.8 %convolution_add_fusion.4 = f32[40,16384]{1,0:T(8,128)S(1)} fusion(f32[8,8,128,128]{3,2,1,0:T(8,128)} %bitcast.216, f32[40,16384]{1,0:T(8,128)S(1)} %copy-done.2, pred[]{:T(512)S(6)} %compare.3, s32[64]{0:T(128)S(1)} %eq.53, pred[64]{0:T(512)(128)(4,1)S(1)} %and.34), kind=kOutput, calls=%fused_computation.3.clone.1 | convolution fusion | flops 504632320 | bytes 9437505 | tf_op jit(solution)/shard_map/while/body/eval_jaxpr/dot_general | solution.py:118
  203.0 5.4 %collective-permute-start.14 = (bf16[1024,128]{1,0:T(8,128)(2,1)}, bf16[1024,128]{1,0:T(8,128)(2,1)}, u32[]{:S(2)}, u32[]{:S(2)}) collective-permute-start(bf16[1024,128]{1,0:T(8,128)(2,1)} %convert_element_type.116), channel_id=1, source_target_pairs={{0,8},{8,16},{16,24},{24,32},{32,40},{40,48},{48,56},{56,64},{64,7... | collective-permute-start | bytes 786440 | tf_op jit(solution)/shard_map/ppermute | solution.py:15
  209.3 6.1 %collective-permute-start.15 = (bf16[1024,128]{1,0:T(8,128)(2,1)}, bf16[1024,128]{1,0:T(8,128)(2,1)}, u32[]{:S(2)}, u32[]{:S(2)}) collective-permute-start(bf16[1024,128]{1,0:T(8,128)(2,1)} %convert_element_type.118), channel_id=1, source_target_pairs={{0,16},{8,24},{16,32},{24,40},{32,48},{40,56},{48,64},{56,72},{64,... | collective-permute-start | bytes 786440 | tf_op jit(solution)/shard_map/ppermute | solution.py:15
  221.4 4.9 %collective-permute-start.10 = (bf16[1024,128]{1,0:T(8,128)(2,1)}, bf16[1024,128]{1,0:T(8,128)(2,1)S(1)}, u32[]{:S(2)}, u32[]{:S(2)}) collective-permute-start(bf16[1024,128]{1,0:T(8,128)(2,1)} %convert_element_type.107), channel_id=1, source_target_pairs={{0,8},{8,16},{16,24},{24,32},{32,40},{40,48},{48,56},{56,64},{64,7... | collective-permute-start | bytes 786440 | tf_op jit(solution)/shard_map/ppermute | solution.py:15
  230.8 5.8 %all-to-all-start.4 = ((bf16[8,128,128]{2,1,0:T(8,128)(2,1)}), bf16[8,128,128]{2,1,0:T(8,128)(2,1)S(1)}, u32[]{:S(2)}, u32[]{:S(2)}) async-start(bf16[8,128,128]{2,1,0:T(8,128)(2,1)} %bitcast.17), calls=%async_computation.4 | async-start | bytes 524288 | tf_op jit(solution)/shard_map/all_to_all | solution.py:148
  243.4 5.1 %all-to-all-start.6 = ((bf16[8,128,128]{2,1,0:T(8,128)(2,1)}), bf16[8,128,128]{2,1,0:T(8,128)(2,1)S(1)}, u32[]{:S(2)}, u32[]{:S(2)}) async-start(bf16[8,128,128]{2,1,0:T(8,128)(2,1)} %bitcast.23), calls=%async_computation.6 | async-start | bytes 524288 | tf_op jit(solution)/shard_map/all_to_all | solution.py:150
  251.0 7.2 %collective-permute-done.9 = bf16[1024,128]{1,0:T(8,128)(2,1)S(1)} collective-permute-done((bf16[1024,128]{1,0:T(8,128)(2,1)S(1)}, bf16[1024,128]{1,0:T(8,128)(2,1)S(1)}, u32[]{:S(2)}, u32[]{:S(2)}) %collective-permute-start.9) | collective-permute-done | bytes 262176 | tf_op jit(solution)/shard_map/ppermute | solution.py:15
  259.0 5.4 %all-to-all-start.5 = ((bf16[8,128,128]{2,1,0:T(8,128)(2,1)}), bf16[8,128,128]{2,1,0:T(8,128)(2,1)S(1)}, u32[]{:S(2)}, u32[]{:S(2)}) async-start(bf16[8,128,128]{2,1,0:T(8,128)(2,1)} %bitcast.20), calls=%async_computation.5 | async-start | bytes 524288 | tf_op jit(solution)/shard_map/all_to_all | solution.py:149
  266.5 4.4 %all-to-all-done.5 = bf16[8,128,128]{2,1,0:T(8,128)(2,1)S(1)} async-done(((bf16[8,128,128]{2,1,0:T(8,128)(2,1)}), bf16[8,128,128]{2,1,0:T(8,128)(2,1)S(1)}, u32[]{:S(2)}, u32[]{:S(2)}) %all-to-all-start.5) | async-done | bytes 262176 | tf_op jit(solution)/shard_map/all_to_all | solution.py:149
  (168 shorter events, 133.1 us)
Async XLA Ops:
  0.6 23.5 %copy-start.9 = (s32[8,16]{1,0:T(8,128)S(1)}, s32[8,16]{1,0:T(8,128)}, u32[]{:S(2)}) copy-start(s32[8,16]{1,0:T(8,128)} %param.13) | copy-start | bytes 1540
  2.6 13.1 %all-to-all-start = ((bf16[128,8,128]{2,0,1:T(8,128)(2,1)}), bf16[128,8,128]{2,0,1:T(8,128)(2,1)S(1)}, u32[]{:S(2)}, u32[]{:S(2)}) async-start(bf16[128,8,128]{2,0,1:T(8,128)(2,1)} %copy.108), calls=%async_computation | async-start | bytes 524288 | tf_op jit(solution)/shard_map/all_to_all | solution.py:25
  15.7 21.6 %all-to-all-start.2 = ((bf16[128,8,128]{2,0,1:T(8,128)(2,1)}), bf16[128,8,128]{2,0,1:T(8,128)(2,1)S(1)}, u32[]{:S(2)}, u32[]{:S(2)}) async-start(bf16[128,8,128]{2,0,1:T(8,128)(2,1)} %copy.112), calls=%async_computation.2 | async-start | bytes 524288 | tf_op jit(solution)/shard_map/all_to_all | solution.py:26
  20.1 28.7 %collective-permute-start = (bf16[1024,128]{1,0:T(8,128)(2,1)S(1)}, bf16[1024,128]{1,0:T(8,128)(2,1)S(1)}, u32[]{:S(2)}, u32[]{:S(2)}) collective-permute-start(bf16[1024,128]{1,0:T(8,128)(2,1)S(1)} %bitcast.225), channel_id=1, source_target_pairs={{0,16},{8,24},{16,32},{24,40},{32,48},{40,56},{48,64},{56,72},{64,... | collective-permute-start | bytes 786440 | tf_op jit(solution)/shard_map/ppermute | solution.py:15
  32.4 20.4 %collective-permute-start.1 = (bf16[1024,128]{1,0:T(8,128)(2,1)S(1)}, bf16[1024,128]{1,0:T(8,128)(2,1)S(1)}, u32[]{:S(2)}, u32[]{:S(2)}) collective-permute-start(bf16[1024,128]{1,0:T(8,128)(2,1)S(1)} %bitcast.226), channel_id=1, source_target_pairs={{0,8},{8,16},{16,24},{24,32},{32,40},{40,48},{48,56},{56,64},{64,7... | collective-permute-start | bytes 786440 | tf_op jit(solution)/shard_map/ppermute | solution.py:15
  34.7 26.0 %collective-permute-start.2 = (bf16[1024,128]{1,0:T(8,128)(2,1)S(1)}, bf16[1024,128]{1,0:T(8,128)(2,1)}, u32[]{:S(2)}, u32[]{:S(2)}) collective-permute-start(bf16[1024,128]{1,0:T(8,128)(2,1)S(1)} %bitcast.227), channel_id=1, source_target_pairs={{8,0},{16,8},{24,16},{32,24},{40,32},{48,40},{56,48},{64,56},{72,6... | collective-permute-start | bytes 786440 | tf_op jit(solution)/shard_map/ppermute | solution.py:15
  36.0 25.7 %collective-permute-start.3 = (bf16[1024,128]{1,0:T(8,128)(2,1)S(1)}, bf16[1024,128]{1,0:T(8,128)(2,1)}, u32[]{:S(2)}, u32[]{:S(2)}) collective-permute-start(bf16[1024,128]{1,0:T(8,128)(2,1)S(1)} %bitcast.228), channel_id=1, source_target_pairs={{16,0},{24,8},{32,16},{40,24},{48,32},{56,40},{64,48},{72,56},{80,... | collective-permute-start | bytes 786440 | tf_op jit(solution)/shard_map/ppermute | solution.py:15
  37.3 29.4 %all-to-all-start.3 = ((bf16[128,8,128]{0,2,1:T(8,128)(2,1)}), bf16[128,8,128]{0,2,1:T(8,128)(2,1)S(1)}, u32[]{:S(2)}, u32[]{:S(2)}) async-start(bf16[128,8,128]{0,2,1:T(8,128)(2,1)} %bitcast.14), calls=%async_computation.3 | async-start | bytes 524288 | tf_op jit(solution)/shard_map/all_to_all | solution.py:27
  42.7 16.7 %collective-permute-start.4 = (bf16[1024,128]{1,0:T(8,128)(2,1)S(1)}, bf16[1024,128]{1,0:T(8,128)(2,1)S(1)}, u32[]{:S(2)}, u32[]{:S(2)}) collective-permute-start(bf16[1024,128]{1,0:T(8,128)(2,1)S(1)} %bitcast.220), channel_id=1, source_target_pairs={{0,16},{8,24},{16,32},{24,40},{32,48},{40,56},{48,64},{56,72},{64,... | collective-permute-start | bytes 786440 | tf_op jit(solution)/shard_map/ppermute | solution.py:15
  48.8 16.2 %collective-permute-start.5 = (bf16[1024,128]{1,0:T(8,128)(2,1)S(1)}, bf16[1024,128]{1,0:T(8,128)(2,1)S(1)}, u32[]{:S(2)}, u32[]{:S(2)}) collective-permute-start(bf16[1024,128]{1,0:T(8,128)(2,1)S(1)} %bitcast.221), channel_id=1, source_target_pairs={{0,8},{8,16},{16,24},{24,32},{32,40},{40,48},{48,56},{56,64},{64,7... | collective-permute-start | bytes 786440 | tf_op jit(solution)/shard_map/ppermute | solution.py:15
  52.9 18.8 %collective-permute-start.6 = (bf16[1024,128]{1,0:T(8,128)(2,1)S(1)}, bf16[1024,128]{1,0:T(8,128)(2,1)}, u32[]{:S(2)}, u32[]{:S(2)}) collective-permute-start(bf16[1024,128]{1,0:T(8,128)(2,1)S(1)} %bitcast.222), channel_id=1, source_target_pairs={{8,0},{16,8},{24,16},{32,24},{40,32},{48,40},{56,48},{64,56},{72,6... | collective-permute-start | bytes 786440 | tf_op jit(solution)/shard_map/ppermute | solution.py:15
  59.4 13.2 %collective-permute-start.7 = (bf16[1024,128]{1,0:T(8,128)(2,1)S(1)}, bf16[1024,128]{1,0:T(8,128)(2,1)}, u32[]{:S(2)}, u32[]{:S(2)}) collective-permute-start(bf16[1024,128]{1,0:T(8,128)(2,1)S(1)} %bitcast.223), channel_id=1, source_target_pairs={{16,0},{24,8},{32,16},{40,24},{48,32},{56,40},{64,48},{72,56},{80,... | collective-permute-start | bytes 786440 | tf_op jit(solution)/shard_map/ppermute | solution.py:15
  66.8 11.4 %all-to-all-start.1 = ((bf16[128,8,128]{0,2,1:T(8,128)(2,1)}), bf16[128,8,128]{0,2,1:T(8,128)(2,1)S(1)}, u32[]{:S(2)}, u32[]{:S(2)}) async-start(bf16[128,8,128]{0,2,1:T(8,128)(2,1)} %bitcast.230), calls=%async_computation.1 | async-start | bytes 524288 | tf_op jit(solution)/shard_map/all_to_all | solution.py:24
  198.8 37.8 %collective-permute-start.12 = (bf16[1024,128]{1,0:T(8,128)(2,1)}, bf16[1024,128]{1,0:T(8,128)(2,1)}, u32[]{:S(2)}, u32[]{:S(2)}) collective-permute-start(bf16[1024,128]{1,0:T(8,128)(2,1)} %convert_element_type.112), channel_id=1, source_target_pairs={{16,0},{24,8},{32,16},{40,24},{48,32},{56,40},{64,48},{72,56},{80,... | collective-permute-start | bytes 786440 | tf_op jit(solution)/shard_map/ppermute | solution.py:15
  200.9 37.8 %collective-permute-start.13 = (bf16[1024,128]{1,0:T(8,128)(2,1)}, bf16[1024,128]{1,0:T(8,128)(2,1)}, u32[]{:S(2)}, u32[]{:S(2)}) collective-permute-start(bf16[1024,128]{1,0:T(8,128)(2,1)} %convert_element_type.114), channel_id=1, source_target_pairs={{8,0},{16,8},{24,16},{32,24},{40,32},{48,40},{56,48},{64,56},{72,6... | collective-permute-start | bytes 786440 | tf_op jit(solution)/shard_map/ppermute | solution.py:15
  203.0 37.0 %collective-permute-start.14 = (bf16[1024,128]{1,0:T(8,128)(2,1)}, bf16[1024,128]{1,0:T(8,128)(2,1)}, u32[]{:S(2)}, u32[]{:S(2)}) collective-permute-start(bf16[1024,128]{1,0:T(8,128)(2,1)} %convert_element_type.116), channel_id=1, source_target_pairs={{0,8},{8,16},{16,24},{24,32},{32,40},{40,48},{48,56},{56,64},{64,7... | collective-permute-start | bytes 786440 | tf_op jit(solution)/shard_map/ppermute | solution.py:15
  209.3 32.0 %collective-permute-start.15 = (bf16[1024,128]{1,0:T(8,128)(2,1)}, bf16[1024,128]{1,0:T(8,128)(2,1)}, u32[]{:S(2)}, u32[]{:S(2)}) collective-permute-start(bf16[1024,128]{1,0:T(8,128)(2,1)} %convert_element_type.118), channel_id=1, source_target_pairs={{0,16},{8,24},{16,32},{24,40},{32,48},{40,56},{48,64},{56,72},{64,... | collective-permute-start | bytes 786440 | tf_op jit(solution)/shard_map/ppermute | solution.py:15
  221.4 27.1 %collective-permute-start.10 = (bf16[1024,128]{1,0:T(8,128)(2,1)}, bf16[1024,128]{1,0:T(8,128)(2,1)S(1)}, u32[]{:S(2)}, u32[]{:S(2)}) collective-permute-start(bf16[1024,128]{1,0:T(8,128)(2,1)} %convert_element_type.107), channel_id=1, source_target_pairs={{0,8},{8,16},{16,24},{24,32},{32,40},{40,48},{48,56},{56,64},{64,7... | collective-permute-start | bytes 786440 | tf_op jit(solution)/shard_map/ppermute | solution.py:15
  230.8 12.5 %all-to-all-start.4 = ((bf16[8,128,128]{2,1,0:T(8,128)(2,1)}), bf16[8,128,128]{2,1,0:T(8,128)(2,1)S(1)}, u32[]{:S(2)}, u32[]{:S(2)}) async-start(bf16[8,128,128]{2,1,0:T(8,128)(2,1)} %bitcast.17), calls=%async_computation.4 | async-start | bytes 524288 | tf_op jit(solution)/shard_map/all_to_all | solution.py:148
  236.6 11.9 %collective-permute-start.11 = (bf16[1024,128]{1,0:T(8,128)(2,1)}, bf16[1024,128]{1,0:T(8,128)(2,1)S(1)}, u32[]{:S(2)}, u32[]{:S(2)}) collective-permute-start(bf16[1024,128]{1,0:T(8,128)(2,1)} %convert_element_type.109), channel_id=1, source_target_pairs={{0,16},{8,24},{16,32},{24,40},{32,48},{40,56},{48,64},{56,72},{64,... | collective-permute-start | bytes 786440 | tf_op jit(solution)/shard_map/ppermute | solution.py:15
  238.7 12.3 %collective-permute-start.8 = (bf16[1024,128]{1,0:T(8,128)(2,1)}, bf16[1024,128]{1,0:T(8,128)(2,1)S(1)}, u32[]{:S(2)}, u32[]{:S(2)}) collective-permute-start(bf16[1024,128]{1,0:T(8,128)(2,1)} %convert_element_type.103), channel_id=1, source_target_pairs={{16,0},{24,8},{32,16},{40,24},{48,32},{56,40},{64,48},{72,56},{80,... | collective-permute-start | bytes 786440 | tf_op jit(solution)/shard_map/ppermute | solution.py:15
  240.0 18.1 %collective-permute-start.9 = (bf16[1024,128]{1,0:T(8,128)(2,1)S(1)}, bf16[1024,128]{1,0:T(8,128)(2,1)S(1)}, u32[]{:S(2)}, u32[]{:S(2)}) collective-permute-start(bf16[1024,128]{1,0:T(8,128)(2,1)S(1)} %convert_element_type.105), channel_id=1, source_target_pairs={{8,0},{16,8},{24,16},{32,24},{40,32},{48,40},{56,48},{64,56},{72,6... | collective-permute-start | bytes 786440 | tf_op jit(solution)/shard_map/ppermute | solution.py:15
  243.4 15.6 %all-to-all-start.6 = ((bf16[8,128,128]{2,1,0:T(8,128)(2,1)}), bf16[8,128,128]{2,1,0:T(8,128)(2,1)S(1)}, u32[]{:S(2)}, u32[]{:S(2)}) async-start(bf16[8,128,128]{2,1,0:T(8,128)(2,1)} %bitcast.23), calls=%async_computation.6 | async-start | bytes 524288 | tf_op jit(solution)/shard_map/all_to_all | solution.py:150
  259.0 11.9 %all-to-all-start.5 = ((bf16[8,128,128]{2,1,0:T(8,128)(2,1)}), bf16[8,128,128]{2,1,0:T(8,128)(2,1)S(1)}, u32[]{:S(2)}, u32[]{:S(2)}) async-start(bf16[8,128,128]{2,1,0:T(8,128)(2,1)} %bitcast.20), calls=%async_computation.5 | async-start | bytes 524288 | tf_op jit(solution)/shard_map/all_to_all | solution.py:149
  (14 other events, 68.2 us)
where the time goes:
time: 277 us; the launch traced here: 272 us
  starting transfers between devices  82.6 us (30%)
  local copies, waits for them, and re-layouts  70.3 us (25%)
  matrix products  67.7 us (24%)
  waiting for transfers between devices  29 us (10%)
  other arithmetic  20.9 us (8%)
    ppermute x16, starting transfers between devices, shifted(): return lax.ppermute(array, axis, pairs)  45.2 us
    ppermute x16, waiting for transfers between devices, shifted(): return lax.ppermute(array, axis, pairs)  17.2 us
    dot_general x2, matrix products, advance(): jnp.dot(live.T, part_v, precision=lax.Precision.HIGHEST, preferred_elemen...  16.7 us
    dot_general x2, matrix products, advance(): jnp.dot(live.T, part_k, precision=lax.Precision.HIGHEST, preferred_elemen...  15.6 us
    unnamed x24, local copies, waits for them, and re-layouts  13.5 us
    concatenate x2, local copies, waits for them, and re-layouts, advance(): jnp.concatenate(part_k_heads, axis=-1).reshape(group * NB, CL * width)  11.1 us
    concatenate x2, local copies, waits for them, and re-layouts, advance(): jnp.concatenate(part_v_heads, axis=-1).reshape(group * NB, CL * width)  10.8 us
    while x24, local copies, waits for them, and re-layouts  9.82 us
  transfers between devices with their start and end apart: 23, of which 7 were waited for; matrix products, arithmetic and copies ran while one was open for 13% of the time, Pallas kernels for 0%

commit v1 on v0

v1 whole, which is shorter than its diff:
```python
import functools

import jax
import jax.numpy as jnp
from jax import lax
from jax.experimental import pallas as pl
from jax.experimental.pallas import tpu as pltpu
from jax.sharding import PartitionSpec as P

CL=128; NB=16; CPN=8; NEAR=40; HDIM=64
NT = (((1,), (1,)), ((), ()))
TN = (((0,), (0,)), ((), ()))
NN = (((1,), (0,)), ((), ()))

def two_heads(x):
    lane = lax.broadcasted_iota(jnp.int32, x.shape, 1)
    zero = jnp.zeros_like(x)
    return jnp.concatenate([jnp.where(lane < HDIM, x, zero), jnp.where(lane < HDIM, zero, x)], axis=0)

def dot(a, b, dims):
    return lax.dot_general(a, b, dims, preferred_element_type=jnp.float32)

def fold(x, op):
    return op(x.reshape(x.shape[0] // 8, 8, x.shape[1]), axis=0)

def attend_kernel(idx_ref, q_ref, g_ref, b_ref, k_ref, v_ref, gq_ref, gk_ref, gv_ref, kg, vg, s, dp, acck, accv, *, CH):
    i = pl.program_id(0)
    @pl.when(i == 0)
    def _():
        acck[...] = jnp.zeros_like(acck)
        accv[...] = jnp.zeros_like(accv)
    q2 = two_heads(q_ref[0] * jnp.bfloat16(0.125))
    g2 = two_heads(g_ref[0])
    R = CH * CL
    def slot(j):
        raw = idx_ref[i * NB + j]
        return jnp.where(raw < 0, 16 + i, raw), jnp.where(raw < 0, jnp.float32(-1e30), jnp.float32(0))
    def first(c, top):
        pens = []
        for u in range(CH):
            at, pen = slot(c * CH + u)
            pens.append(pen)
            kg[pl.ds(pl.multiple_of(c * R + u * CL, CL), CL), :] = k_ref[at]
            vg[pl.ds(pl.multiple_of(c * R + u * CL, CL), CL), :] = v_ref[at]
        rows = pl.ds(pl.multiple_of(c * R, R), R)
        st = dot(kg[rows, :], q2, NT)
        for u in range(CH):
            bt = b_ref[0, c * CH + u].astype(jnp.float32).T + pens[u]
            x = st[u * CL:(u + 1) * CL] + jnp.concatenate([bt, bt], axis=1)
            s[pl.ds(pl.multiple_of(c * R + u * CL, CL), CL), :] = x
            top = jnp.maximum(top, fold(x, jnp.max))
        return top
    top = lax.fori_loop(0, NB // CH, first, jnp.full((8, 2 * CL), -jnp.inf, jnp.float32))
    top = jnp.max(top, axis=0, keepdims=True)
    def second(c, carry):
        total, delta = carry
        rows = pl.ds(pl.multiple_of(c * R, R), R)
        d = dot(vg[rows, :], g2, NT)
        e = jnp.exp(s[rows, :] - top)
        s[rows, :] = e
        dp[rows, :] = d
        return total + fold(e, jnp.sum), delta + fold(e * d, jnp.sum)
    zero = jnp.zeros((8, 2 * CL), jnp.float32)
    total, delta = lax.fori_loop(0, NB // CH, second, (zero, zero))
    inv = 1.0 / jnp.sum(total, axis=0, keepdims=True)
    delta = jnp.sum(delta, axis=0, keepdims=True) * inv
    def third(c, gqt):
        rows = pl.ds(pl.multiple_of(c * R, R), R)
        p = s[rows, :] * inv
        ph = p.astype(jnp.bfloat16)
        ds = (p * (dp[rows, :] - delta)).astype(jnp.bfloat16)
        pv = dot(ph, g2, NN)
        pk = dot(ds, q2, NN)
        for u in range(CH):
            at, _ = slot(c * CH + u)
            accv[at] += pv[u * CL:(u + 1) * CL]
            acck[at] += pk[u * CL:(u + 1) * CL]
        return gqt + dot(kg[rows, :], ds, TN)
    gqt = lax.fori_loop(0, NB // CH, third, jnp.zeros((CL, 2 * CL), jnp.float32))
    gqt = jnp.concatenate([gqt[:HDIM, :CL], gqt[HDIM:, CL:]], axis=0) * 0.125
    gq_ref[0] = gqt.T.astype(jnp.bfloat16)
    @pl.when(i == CPN - 1)
    def _():
        gk_ref[...] = acck[...].astype(jnp.bfloat16)
        gv_ref[...] = accv[...].astype(jnp.bfloat16)

def attend(index, q, g, bias, near_k, near_v, CH=8):
    bf = jnp.bfloat16
    whole = pl.BlockSpec((NEAR, CL, CL), lambda i, x: (0, 0, 0), pipeline_mode=pl.Buffered(1))
    one = pl.BlockSpec((1, CL, CL), lambda i, x: (i, 0, 0))
    return pl.pallas_call(
        functools.partial(attend_kernel, CH=CH),
        out_shape=(jax.ShapeDtypeStruct((CPN, CL, CL), bf), jax.ShapeDtypeStruct((NEAR, CL, CL), bf), jax.ShapeDtypeStruct((NEAR, CL, CL), bf)),
        grid_spec=pltpu.PrefetchScalarGridSpec(
            num_scalar_prefetch=1, grid=(CPN,),
            in_specs=[one, one, pl.BlockSpec((1, NB, CL, CL), lambda i, x: (i, 0, 0, 0)), whole, whole],
            out_specs=[one, whole, whole],
            scratch_shapes=[pltpu.VMEM((NB * CL, CL), bf), pltpu.VMEM((NB * CL, CL), bf), pltpu.VMEM((NB * CL, 2 * CL), jnp.float32), pltpu.VMEM((NB * CL, 2 * CL), jnp.float32), pltpu.VMEM((NEAR, CL, CL), jnp.float32), pltpu.VMEM((NEAR, CL, CL), jnp.float32)]),
        compiler_params=pltpu.CompilerParams(dimension_semantics=("arbitrary",)),
    )(index, q, g, bias, near_k, near_v)


REACH = 2


def shifted(array, axis, by):
    size = lax.axis_size(axis)
    pairs = [(i, i + by) for i in range(size) if 0 <= i + by < size]
    return lax.ppermute(array, axis, pairs)


def on_device(query_rows, key_rows, value_rows, grad_out, heat_bias, block_pattern):
    def enter(a):
        return lax.all_to_all(a, "head", split_axis=1, concat_axis=0, tiled=True).reshape(CPN, CL, CL)

    def leave(a):
        return lax.all_to_all(a.reshape(CPN * CL, CL), "head", split_axis=0, concat_axis=1, tiled=True)

    k, v, q, g = enter(key_rows), enter(value_rows), enter(query_rows), enter(grad_out)
    shard = lax.axis_index("node")
    offsets = list(range(-REACH, REACH + 1))
    near_k = jnp.concatenate([k if o == 0 else shifted(k, "node", -o) for o in offsets], axis=0)
    near_v = jnp.concatenate([v if o == 0 else shifted(v, "node", -o) for o in offsets], axis=0)
    index = jnp.where(block_pattern < 0, -1, block_pattern - (shard - REACH) * CPN).reshape(-1)
    gq, gk, gv = attend(index, q, g, heat_bias, near_k, near_v)

    def total(parts):
        acc = parts[REACH * CPN : (REACH + 1) * CPN].astype(jnp.float32)
        for o in offsets:
            if o != 0:
                first = (o + REACH) * CPN
                acc = acc + shifted(parts[first : first + CPN], "node", o).astype(jnp.float32)
        return acc.astype(jnp.bfloat16)

    return leave(gq), leave(total(gk)), leave(total(gv))


def solution(mesh):
    rows = P(("node", "head"), None)
    return jax.shard_map(
        on_device,
        mesh=mesh,
        in_specs=(rows, rows, rows, rows, P("node", None, None, None), P("node", None)),
        out_specs=(rows, rows, rows),
        check_vma=False,
    )
```

time: 277 us -> 177 us (0.64)
  the two profiles are of different devices: /device:TPU:1 before, /device:TPU:128 now
where the time goes in v1:
time: 177 us; the launch traced here: 176 us
  starting transfers between devices  96.6 us (55%)
  waiting for transfers between devices  30.4 us (17%)
  Pallas kernels  26.3 us (15%)
  local copies, waits for them, and re-layouts  17.5 us (10%)
  other arithmetic  3.66 us (2%)
    ppermute x16, starting transfers between devices, shifted(): return lax.ppermute(array, axis, pairs)  68.4 us
    pallas_call x1, Pallas kernels, attend(): pl.pallas_call(functools.partial(attend_kernel, CH=CH), out_shape=(jax.Sh...  26.3 us
    all_to_all x4, starting transfers between devices, enter(): lax.all_to_all(a, 'head', split_axis=1, concat_axis=0, tiled=True)  16.6 us
    all_to_all x4, waiting for transfers between devices, enter(): lax.all_to_all(a, 'head', split_axis=1, concat_axis=0, tiled=True)  12 us
    all_to_all x3, starting transfers between devices, leave(): lax.all_to_all(a.reshape(CPN * CL, CL), 'head', split_axis=0, concat_axis...  11.5 us
    all_to_all x3, waiting for transfers between devices, leave(): lax.all_to_all(a.reshape(CPN * CL, CL), 'head', split_axis=0, concat_axis...  10.6 us
    unnamed x35, local copies, waits for them, and re-layouts  8.76 us
    ppermute x16, waiting for transfers between devices, shifted(): return lax.ppermute(array, axis, pairs)  7.85 us
  transfers between devices with their start and end apart: 23, of which 7 were waited for; matrix products, arithmetic and copies ran while one was open for 8% of the time, Pallas kernels for 0%

profile of v1, /device:TPU:128, one launch (start us, length us, event | category | flops | bytes accessed | tf_op | source)
XLA Modules:
  0.0 175.6 jit_solution(1650808179845693271)
XLA Ops:
  2.7 4.3 %all-to-all-start.2 = ((bf16[128,8,128]{2,0,1:T(8,128)(2,1)}), bf16[128,8,128]{2,0,1:T(8,128)(2,1)S(1)}, u32[]{:S(2)}, u32[]{:S(2)}) async-start(bf16[128,8,128]{2,0,1:T(8,128)(2,1)} %copy.14), calls=%async_computation.2 | async-start | bytes 524288 | tf_op jit(solution)/shard_map/all_to_all | solution.py:114
  8.0 6.5 %all-to-all-done.2 = bf16[128,8,128]{2,0,1:T(8,128)(2,1)S(1)} async-done(((bf16[128,8,128]{2,0,1:T(8,128)(2,1)}), bf16[128,8,128]{2,0,1:T(8,128)(2,1)S(1)}, u32[]{:S(2)}, u32[]{:S(2)}) %all-to-all-start.2) | async-done | bytes 262176 | tf_op jit(solution)/shard_map/all_to_all | solution.py:114
  14.5 3.4 %all-to-all-start.3 = ((bf16[128,8,128]{2,0,1:T(8,128)(2,1)}), bf16[128,8,128]{2,0,1:T(8,128)(2,1)S(1)}, u32[]{:S(2)}, u32[]{:S(2)}) async-start(bf16[128,8,128]{2,0,1:T(8,128)(2,1)} %copy.16), calls=%async_computation.3 | async-start | bytes 524288 | tf_op jit(solution)/shard_map/all_to_all | solution.py:114
  17.9 5.1 %collective-permute-start = (bf16[8,128,128]{2,1,0:T(8,128)(2,1)S(1)}, bf16[8,128,128]{2,1,0:T(8,128)(2,1)S(1)}, u32[]{:S(2)}, u32[]{:S(2)}) collective-permute-start(bf16[8,128,128]{2,1,0:T(8,128)(2,1)S(1)} %bitcast.20), channel_id=1, source_target_pairs={{0,16},{8,24},{16,32},{24,40},{32,48},{40,56},{48,64},{56,72},{64,... | collective-permute-start | bytes 786440 | tf_op jit(solution)/shard_map/ppermute | solution.py:109
  26.7 4.7 %all-to-all-start = ((bf16[128,8,128]{2,0,1:T(8,128)(2,1)}), bf16[128,8,128]{2,0,1:T(8,128)(2,1)S(1)}, u32[]{:S(2)}, u32[]{:S(2)}) async-start(bf16[128,8,128]{2,0,1:T(8,128)(2,1)} %copy.10), calls=%async_computation | async-start | bytes 524288 | tf_op jit(solution)/shard_map/all_to_all | solution.py:114
  31.4 4.2 %collective-permute-start.4 = (bf16[8,128,128]{2,1,0:T(8,128)(2,1)S(1)}, bf16[8,128,128]{2,1,0:T(8,128)(2,1)S(1)}, u32[]{:S(2)}, u32[]{:S(2)}) collective-permute-start(bf16[8,128,128]{2,1,0:T(8,128)(2,1)S(1)} %bitcast.16), channel_id=1, source_target_pairs={{0,16},{8,24},{16,32},{24,40},{32,48},{40,56},{48,64},{56,72},{64,... | collective-permute-start | bytes 786440 | tf_op jit(solution)/shard_map/ppermute | solution.py:109
  37.3 5.2 %collective-permute-start.7 = (bf16[8,128,128]{2,1,0:T(8,128)(2,1)S(1)}, bf16[8,128,128]{2,1,0:T(8,128)(2,1)}, u32[]{:S(2)}, u32[]{:S(2)}) collective-permute-start(bf16[8,128,128]{2,1,0:T(8,128)(2,1)S(1)} %bitcast.17), channel_id=1, source_target_pairs={{16,0},{24,8},{32,16},{40,24},{48,32},{56,40},{64,48},{72,56},{80,... | collective-permute-start | bytes 786440 | tf_op jit(solution)/shard_map/ppermute | solution.py:109
  42.5 4.5 %collective-permute-start.6 = (bf16[8,128,128]{2,1,0:T(8,128)(2,1)S(1)}, bf16[8,128,128]{2,1,0:T(8,128)(2,1)}, u32[]{:S(2)}, u32[]{:S(2)}) collective-permute-start(bf16[8,128,128]{2,1,0:T(8,128)(2,1)S(1)} %bitcast.18), channel_id=1, source_target_pairs={{8,0},{16,8},{24,16},{32,24},{40,32},{48,40},{56,48},{64,56},{72,6... | collective-permute-start | bytes 786440 | tf_op jit(solution)/shard_map/ppermute | solution.py:109
  54.0 5.8 %collective-permute-start.2 = (bf16[8,128,128]{2,1,0:T(8,128)(2,1)S(1)}, bf16[8,128,128]{2,1,0:T(8,128)(2,1)S(1)}, u32[]{:S(2)}, u32[]{:S(2)}) collective-permute-start(bf16[8,128,128]{2,1,0:T(8,128)(2,1)S(1)} %bitcast.23), channel_id=1, source_target_pairs={{8,0},{16,8},{24,16},{32,24},{40,32},{48,40},{56,48},{64,56},{72,6... | collective-permute-start | bytes 786440 | tf_op jit(solution)/shard_map/ppermute | solution.py:109
  62.6 5.6 %collective-permute-done.2 = bf16[8,128,128]{2,1,0:T(8,128)(2,1)S(1)} collective-permute-done((bf16[8,128,128]{2,1,0:T(8,128)(2,1)S(1)}, bf16[8,128,128]{2,1,0:T(8,128)(2,1)S(1)}, u32[]{:S(2)}, u32[]{:S(2)}) %collective-permute-start.2) | collective-permute-done | bytes 262176 | tf_op jit(solution)/shard_map/ppermute | solution.py:109
  68.4 4.2 %all-to-all-start.1 = ((bf16[128,8,128]{2,0,1:T(8,128)(2,1)}), bf16[128,8,128]{2,0,1:T(8,128)(2,1)S(1)}, u32[]{:S(2)}, u32[]{:S(2)}) async-start(bf16[128,8,128]{2,0,1:T(8,128)(2,1)} %copy.12), calls=%async_computation.1 | async-start | bytes 524288 | tf_op jit(solution)/shard_map/all_to_all | solution.py:114
  74.6 5.5 %all-to-all-done.1 = bf16[128,8,128]{2,0,1:T(8,128)(2,1)S(1)} async-done(((bf16[128,8,128]{2,0,1:T(8,128)(2,1)}), bf16[128,8,128]{2,0,1:T(8,128)(2,1)S(1)}, u32[]{:S(2)}, u32[]{:S(2)}) %all-to-all-start.1) | async-done | bytes 262176 | tf_op jit(solution)/shard_map/all_to_all | solution.py:114
  80.8 26.3 %shard_map.85 = (bf16[8,128,128]{2,1,0:T(8,128)(2,1)}, bf16[40,128,128]{2,1,0:T(8,128)(2,1)}, bf16[40,128,128]{2,1,0:T(8,128)(2,1)}) custom-call(s32[128]{0:T(128)} %reshape.44.idx_ref, bf16[8,128,128]{2,1,0:T(8,128)(2,1)} %bitcast.34, bf16[8,128,128]{2,1,0:T(8,128)(2,1)} %bitcast.35, bf16[8,16,128,128]{3,2,1,0:T(8,128)(2,1)} %b_ref.1, ...), custom_call_target="tpu_custom_call" | custom-call | tf_op jit(solution)/shard_map/pallas_call | solution.py:91
  109.3 3.9 %collective-permute-start.8 = (bf16[8,128,128]{2,1,0:T(8,128)(2,1)S(1)}, bf16[8,128,128]{2,1,0:T(8,128)(2,1)S(1)}, u32[]{:S(2)}, u32[]{:S(2)}) collective-permute-start(bf16[8,128,128]{2,1,0:T(8,128)(2,1)S(1)} %get-tuple-element.16), channel_id=1, source_target_pairs={{16,0},{24,8},{32,16},{40,24},{48,32},{56,40},{64,48},{72,56},{80,... | collective-permute-start | bytes 786440 | tf_op jit(solution)/shard_map/ppermute | solution.py:109
  113.2 3.4 %collective-permute-start.11 = (bf16[8,128,128]{2,1,0:T(8,128)(2,1)S(1)}, bf16[8,128,128]{2,1,0:T(8,128)(2,1)S(1)}, u32[]{:S(2)}, u32[]{:S(2)}) collective-permute-start(bf16[8,128,128]{2,1,0:T(8,128)(2,1)S(1)} %get-tuple-element.17), channel_id=1, source_target_pairs={{0,16},{8,24},{16,32},{24,40},{32,48},{40,56},{48,64},{56,72},{64,... | collective-permute-start | bytes 786440 | tf_op jit(solution)/shard_map/ppermute | solution.py:109
  116.6 5.2 %collective-permute-start.10 = (bf16[8,128,128]{2,1,0:T(8,128)(2,1)}, bf16[8,128,128]{2,1,0:T(8,128)(2,1)S(1)}, u32[]{:S(2)}, u32[]{:S(2)}) collective-permute-start(bf16[8,128,128]{2,1,0:T(8,128)(2,1)} %get-tuple-element.18), channel_id=1, source_target_pairs={{0,8},{8,16},{16,24},{24,32},{32,40},{40,48},{48,56},{56,64},{64,7... | collective-permute-start | bytes 786440 | tf_op jit(solution)/shard_map/ppermute | solution.py:109
  121.9 6.7 %collective-permute-start.9 = (bf16[8,128,128]{2,1,0:T(8,128)(2,1)}, bf16[8,128,128]{2,1,0:T(8,128)(2,1)S(1)}, u32[]{:S(2)}, u32[]{:S(2)}) collective-permute-start(bf16[8,128,128]{2,1,0:T(8,128)(2,1)} %get-tuple-element.19), channel_id=1, source_target_pairs={{8,0},{16,8},{24,16},{32,24},{40,32},{48,40},{56,48},{64,56},{72,6... | collective-permute-start | bytes 786440 | tf_op jit(solution)/shard_map/ppermute | solution.py:109
  128.6 3.4 %all-to-all-start.4 = ((bf16[8,128,128]{2,1,0:T(8,128)(2,1)}), bf16[8,128,128]{2,1,0:T(8,128)(2,1)S(1)}, u32[]{:S(2)}, u32[]{:S(2)}) async-start(bf16[8,128,128]{2,1,0:T(8,128)(2,1)} %get-tuple-element.6), calls=%async_computation.4 | async-start | bytes 524288 | tf_op jit(solution)/shard_map/all_to_all | solution.py:117
  136.4 4.0 %collective-permute-start.15 = (bf16[8,128,128]{2,1,0:T(8,128)(2,1)}, bf16[8,128,128]{2,1,0:T(8,128)(2,1)S(1)}, u32[]{:S(2)}, u32[]{:S(2)}) collective-permute-start(bf16[8,128,128]{2,1,0:T(8,128)(2,1)} %get-tuple-element.13), channel_id=1, source_target_pairs={{0,16},{8,24},{16,32},{24,40},{32,48},{40,56},{48,64},{56,72},{64,... | collective-permute-start | bytes 786440 | tf_op jit(solution)/shard_map/ppermute | solution.py:109
  142.3 7.2 %collective-permute-start.13 = (bf16[8,128,128]{2,1,0:T(8,128)(2,1)}, bf16[8,128,128]{2,1,0:T(8,128)(2,1)}, u32[]{:S(2)}, u32[]{:S(2)}) collective-permute-start(bf16[8,128,128]{2,1,0:T(8,128)(2,1)} %get-tuple-element.15), channel_id=1, source_target_pairs={{8,0},{16,8},{24,16},{32,24},{40,32},{48,40},{56,48},{64,56},{72,6... | collective-permute-start | bytes 786440 | tf_op jit(solution)/shard_map/ppermute | solution.py:109
  151.4 4.7 %all-to-all-start.5 = ((bf16[8,128,128]{2,1,0:T(8,128)(2,1)}), bf16[8,128,128]{2,1,0:T(8,128)(2,1)S(1)}, u32[]{:S(2)}, u32[]{:S(2)}) async-start(bf16[8,128,128]{2,1,0:T(8,128)(2,1)} %add_convert_fusion.1), calls=%async_computation.5 | async-start | bytes 524288 | tf_op jit(solution)/shard_map/all_to_all | solution.py:117
  158.5 5.2 %all-to-all-done.5 = bf16[8,128,128]{2,1,0:T(8,128)(2,1)S(1)} async-done(((bf16[8,128,128]{2,1,0:T(8,128)(2,1)}), bf16[8,128,128]{2,1,0:T(8,128)(2,1)S(1)}, u32[]{:S(2)}, u32[]{:S(2)}) %all-to-all-start.5) | async-done | bytes 262176 | tf_op jit(solution)/shard_map/all_to_all | solution.py:117
  163.7 3.4 %all-to-all-start.6 = ((bf16[8,128,128]{2,1,0:T(8,128)(2,1)}), bf16[8,128,128]{2,1,0:T(8,128)(2,1)S(1)}, u32[]{:S(2)}, u32[]{:S(2)}) async-start(bf16[8,128,128]{2,1,0:T(8,128)(2,1)} %add_convert_fusion), calls=%async_computation.6 | async-start | bytes 524288 | tf_op jit(solution)/shard_map/all_to_all | solution.py:117
  169.2 5.4 %all-to-all-done.6 = bf16[8,128,128]{2,1,0:T(8,128)(2,1)S(1)} async-done(((bf16[8,128,128]{2,1,0:T(8,128)(2,1)}), bf16[8,128,128]{2,1,0:T(8,128)(2,1)S(1)}, u32[]{:S(2)}, u32[]{:S(2)}) %all-to-all-start.6) | async-done | bytes 262176 | tf_op jit(solution)/shard_map/all_to_all | solution.py:117
  (73 shorter events, 36.5 us)
Async XLA Ops:
  2.7 11.8 %all-to-all-start.2 = ((bf16[128,8,128]{2,0,1:T(8,128)(2,1)}), bf16[128,8,128]{2,0,1:T(8,128)(2,1)S(1)}, u32[]{:S(2)}, u32[]{:S(2)}) async-start(bf16[128,8,128]{2,0,1:T(8,128)(2,1)} %copy.14), calls=%async_computation.2 | async-start | bytes 524288 | tf_op jit(solution)/shard_map/all_to_all | solution.py:114
  7.2 29.1 %copy-start.7 = (bf16[128,1024]{1,0:T(8,128)(2,1)S(1)}, bf16[128,1024]{1,0:T(8,128)(2,1)}, u32[]{:S(2)}) copy-start(bf16[128,1024]{1,0:T(8,128)(2,1)} %param.9) | copy-start | bytes 786436
  14.5 12.2 %all-to-all-start.3 = ((bf16[128,8,128]{2,0,1:T(8,128)(2,1)}), bf16[128,8,128]{2,0,1:T(8,128)(2,1)S(1)}, u32[]{:S(2)}, u32[]{:S(2)}) async-start(bf16[128,8,128]{2,0,1:T(8,128)(2,1)} %copy.16), calls=%async_computation.3 | async-start | bytes 524288 | tf_op jit(solution)/shard_map/all_to_all | solution.py:114
  17.9 29.1 %collective-permute-start = (bf16[8,128,128]{2,1,0:T(8,128)(2,1)S(1)}, bf16[8,128,128]{2,1,0:T(8,128)(2,1)S(1)}, u32[]{:S(2)}, u32[]{:S(2)}) collective-permute-start(bf16[8,128,128]{2,1,0:T(8,128)(2,1)S(1)} %bitcast.20), channel_id=1, source_target_pairs={{0,16},{8,24},{16,32},{24,40},{32,48},{40,56},{48,64},{56,72},{64,... | collective-permute-start | bytes 786440 | tf_op jit(solution)/shard_map/ppermute | solution.py:109
  24.1 29.9 %collective-permute-start.1 = (bf16[8,128,128]{2,1,0:T(8,128)(2,1)S(1)}, bf16[8,128,128]{2,1,0:T(8,128)(2,1)}, u32[]{:S(2)}, u32[]{:S(2)}) collective-permute-start(bf16[8,128,128]{2,1,0:T(8,128)(2,1)S(1)} %bitcast.21), channel_id=1, source_target_pairs={{0,8},{8,16},{16,24},{24,32},{32,40},{40,48},{48,56},{56,64},{64,7... | collective-permute-start | bytes 786440 | tf_op jit(solution)/shard_map/ppermute | solution.py:109
  26.7 41.6 %all-to-all-start = ((bf16[128,8,128]{2,0,1:T(8,128)(2,1)}), bf16[128,8,128]{2,0,1:T(8,128)(2,1)S(1)}, u32[]{:S(2)}, u32[]{:S(2)}) async-start(bf16[128,8,128]{2,0,1:T(8,128)(2,1)} %copy.10), calls=%async_computation | async-start | bytes 524288 | tf_op jit(solution)/shard_map/all_to_all | solution.py:114
  31.4 17.6 %collective-permute-start.4 = (bf16[8,128,128]{2,1,0:T(8,128)(2,1)S(1)}, bf16[8,128,128]{2,1,0:T(8,128)(2,1)S(1)}, u32[]{:S(2)}, u32[]{:S(2)}) collective-permute-start(bf16[8,128,128]{2,1,0:T(8,128)(2,1)S(1)} %bitcast.16), channel_id=1, source_target_pairs={{0,16},{8,24},{16,32},{24,40},{32,48},{40,56},{48,64},{56,72},{64,... | collective-permute-start | bytes 786440 | tf_op jit(solution)/shard_map/ppermute | solution.py:109
  37.3 36.3 %collective-permute-start.7 = (bf16[8,128,128]{2,1,0:T(8,128)(2,1)S(1)}, bf16[8,128,128]{2,1,0:T(8,128)(2,1)}, u32[]{:S(2)}, u32[]{:S(2)}) collective-permute-start(bf16[8,128,128]{2,1,0:T(8,128)(2,1)S(1)} %bitcast.17), channel_id=1, source_target_pairs={{16,0},{24,8},{32,16},{40,24},{48,32},{56,40},{64,48},{72,56},{80,... | collective-permute-start | bytes 786440 | tf_op jit(solution)/shard_map/ppermute | solution.py:109
  42.5 30.0 %collective-permute-start.6 = (bf16[8,128,128]{2,1,0:T(8,128)(2,1)S(1)}, bf16[8,128,128]{2,1,0:T(8,128)(2,1)}, u32[]{:S(2)}, u32[]{:S(2)}) collective-permute-start(bf16[8,128,128]{2,1,0:T(8,128)(2,1)S(1)} %bitcast.18), channel_id=1, source_target_pairs={{8,0},{16,8},{24,16},{32,24},{40,32},{48,40},{56,48},{64,56},{72,6... | collective-permute-start | bytes 786440 | tf_op jit(solution)/shard_map/ppermute | solution.py:109
  47.0 15.5 %collective-permute-start.5 = (bf16[8,128,128]{2,1,0:T(8,128)(2,1)S(1)}, bf16[8,128,128]{2,1,0:T(8,128)(2,1)S(1)}, u32[]{:S(2)}, u32[]{:S(2)}) collective-permute-start(bf16[8,128,128]{2,1,0:T(8,128)(2,1)S(1)} %bitcast.19), channel_id=1, source_target_pairs={{0,8},{8,16},{16,24},{24,32},{32,40},{40,48},{48,56},{56,64},{64,7... | collective-permute-start | bytes 786440 | tf_op jit(solution)/shard_map/ppermute | solution.py:109
  49.7 18.6 %collective-permute-start.3 = (bf16[8,128,128]{2,1,0:T(8,128)(2,1)S(1)}, bf16[8,128,128]{2,1,0:T(8,128)(2,1)S(1)}, u32[]{:S(2)}, u32[]{:S(2)}) collective-permute-start(bf16[8,128,128]{2,1,0:T(8,128)(2,1)S(1)} %bitcast.22), channel_id=1, source_target_pairs={{16,0},{24,8},{32,16},{40,24},{48,32},{56,40},{64,48},{72,56},{80,... | collective-permute-start | bytes 786440 | tf_op jit(solution)/shard_map/ppermute | solution.py:109
  54.0 14.2 %collective-permute-start.2 = (bf16[8,128,128]{2,1,0:T(8,128)(2,1)S(1)}, bf16[8,128,128]{2,1,0:T(8,128)(2,1)S(1)}, u32[]{:S(2)}, u32[]{:S(2)}) collective-permute-start(bf16[8,128,128]{2,1,0:T(8,128)(2,1)S(1)} %bitcast.23), channel_id=1, source_target_pairs={{8,0},{16,8},{24,16},{32,24},{40,32},{48,40},{56,48},{64,56},{72,6... | collective-permute-start | bytes 786440 | tf_op jit(solution)/shard_map/ppermute | solution.py:109
  68.4 11.7 %all-to-all-start.1 = ((bf16[128,8,128]{2,0,1:T(8,128)(2,1)}), bf16[128,8,128]{2,0,1:T(8,128)(2,1)S(1)}, u32[]{:S(2)}, u32[]{:S(2)}) async-start(bf16[128,8,128]{2,0,1:T(8,128)(2,1)} %copy.12), calls=%async_computation.1 | async-start | bytes 524288 | tf_op jit(solution)/shard_map/all_to_all | solution.py:114
  109.3 27.1 %collective-permute-start.8 = (bf16[8,128,128]{2,1,0:T(8,128)(2,1)S(1)}, bf16[8,128,128]{2,1,0:T(8,128)(2,1)S(1)}, u32[]{:S(2)}, u32[]{:S(2)}) collective-permute-start(bf16[8,128,128]{2,1,0:T(8,128)(2,1)S(1)} %get-tuple-element.16), channel_id=1, source_target_pairs={{16,0},{24,8},{32,16},{40,24},{48,32},{56,40},{64,48},{72,56},{80,... | collective-permute-start | bytes 786440 | tf_op jit(solution)/shard_map/ppermute | solution.py:109
  113.2 27.2 %collective-permute-start.11 = (bf16[8,128,128]{2,1,0:T(8,128)(2,1)S(1)}, bf16[8,128,128]{2,1,0:T(8,128)(2,1)S(1)}, u32[]{:S(2)}, u32[]{:S(2)}) collective-permute-start(bf16[8,128,128]{2,1,0:T(8,128)(2,1)S(1)} %get-tuple-element.17), channel_id=1, source_target_pairs={{0,16},{8,24},{16,32},{24,40},{32,48},{40,56},{48,64},{56,72},{64,... | collective-permute-start | bytes 786440 | tf_op jit(solution)/shard_map/ppermute | solution.py:109
  116.6 25.7 %collective-permute-start.10 = (bf16[8,128,128]{2,1,0:T(8,128)(2,1)}, bf16[8,128,128]{2,1,0:T(8,128)(2,1)S(1)}, u32[]{:S(2)}, u32[]{:S(2)}) collective-permute-start(bf16[8,128,128]{2,1,0:T(8,128)(2,1)} %get-tuple-element.18), channel_id=1, source_target_pairs={{0,8},{8,16},{16,24},{24,32},{32,40},{40,48},{48,56},{56,64},{64,7... | collective-permute-start | bytes 786440 | tf_op jit(solution)/shard_map/ppermute | solution.py:109
  121.9 27.7 %collective-permute-start.9 = (bf16[8,128,128]{2,1,0:T(8,128)(2,1)}, bf16[8,128,128]{2,1,0:T(8,128)(2,1)S(1)}, u32[]{:S(2)}, u32[]{:S(2)}) collective-permute-start(bf16[8,128,128]{2,1,0:T(8,128)(2,1)} %get-tuple-element.19), channel_id=1, source_target_pairs={{8,0},{16,8},{24,16},{32,24},{40,32},{48,40},{56,48},{64,56},{72,6... | collective-permute-start | bytes 786440 | tf_op jit(solution)/shard_map/ppermute | solution.py:109
  128.6 22.9 %all-to-all-start.4 = ((bf16[8,128,128]{2,1,0:T(8,128)(2,1)}), bf16[8,128,128]{2,1,0:T(8,128)(2,1)S(1)}, u32[]{:S(2)}, u32[]{:S(2)}) async-start(bf16[8,128,128]{2,1,0:T(8,128)(2,1)} %get-tuple-element.6), calls=%async_computation.4 | async-start | bytes 524288 | tf_op jit(solution)/shard_map/all_to_all | solution.py:117
  133.0 23.1 %collective-permute-start.12 = (bf16[8,128,128]{2,1,0:T(8,128)(2,1)}, bf16[8,128,128]{2,1,0:T(8,128)(2,1)S(1)}, u32[]{:S(2)}, u32[]{:S(2)}) collective-permute-start(bf16[8,128,128]{2,1,0:T(8,128)(2,1)} %get-tuple-element.12), channel_id=1, source_target_pairs={{16,0},{24,8},{32,16},{40,24},{48,32},{56,40},{64,48},{72,56},{80,... | collective-permute-start | bytes 786440 | tf_op jit(solution)/shard_map/ppermute | solution.py:109
  136.4 19.8 %collective-permute-start.15 = (bf16[8,128,128]{2,1,0:T(8,128)(2,1)}, bf16[8,128,128]{2,1,0:T(8,128)(2,1)S(1)}, u32[]{:S(2)}, u32[]{:S(2)}) collective-permute-start(bf16[8,128,128]{2,1,0:T(8,128)(2,1)} %get-tuple-element.13), channel_id=1, source_target_pairs={{0,16},{8,24},{16,32},{24,40},{32,48},{40,56},{48,64},{56,72},{64,... | collective-permute-start | bytes 786440 | tf_op jit(solution)/shard_map/ppermute | solution.py:109
  140.4 16.3 %collective-permute-start.14 = (bf16[8,128,128]{2,1,0:T(8,128)(2,1)}, bf16[8,128,128]{2,1,0:T(8,128)(2,1)S(1)}, u32[]{:S(2)}, u32[]{:S(2)}) collective-permute-start(bf16[8,128,128]{2,1,0:T(8,128)(2,1)} %get-tuple-element.14), channel_id=1, source_target_pairs={{0,8},{8,16},{16,24},{24,32},{32,40},{40,48},{48,56},{56,64},{64,7... | collective-permute-start | bytes 786440 | tf_op jit(solution)/shard_map/ppermute | solution.py:109
  142.3 14.4 %collective-permute-start.13 = (bf16[8,128,128]{2,1,0:T(8,128)(2,1)}, bf16[8,128,128]{2,1,0:T(8,128)(2,1)}, u32[]{:S(2)}, u32[]{:S(2)}) collective-permute-start(bf16[8,128,128]{2,1,0:T(8,128)(2,1)} %get-tuple-element.15), channel_id=1, source_target_pairs={{8,0},{16,8},{24,16},{32,24},{40,32},{48,40},{56,48},{64,56},{72,6... | collective-permute-start | bytes 786440 | tf_op jit(solution)/shard_map/ppermute | solution.py:109
  151.4 12.3 %all-to-all-start.5 = ((bf16[8,128,128]{2,1,0:T(8,128)(2,1)}), bf16[8,128,128]{2,1,0:T(8,128)(2,1)S(1)}, u32[]{:S(2)}, u32[]{:S(2)}) async-start(bf16[8,128,128]{2,1,0:T(8,128)(2,1)} %add_convert_fusion.1), calls=%async_computation.5 | async-start | bytes 524288 | tf_op jit(solution)/shard_map/all_to_all | solution.py:117
  163.7 10.9 %all-to-all-start.6 = ((bf16[8,128,128]{2,1,0:T(8,128)(2,1)}), bf16[8,128,128]{2,1,0:T(8,128)(2,1)S(1)}, u32[]{:S(2)}, u32[]{:S(2)}) async-start(bf16[8,128,128]{2,1,0:T(8,128)(2,1)} %add_convert_fusion), calls=%async_computation.6 | async-start | bytes 524288 | tf_op jit(solution)/shard_map/all_to_all | solution.py:117
  (9 other events, 111.4 us)

commit v2 on v1

--- a/solution.py
+++ b/solution.py
@@ -101,38 +101,212 @@
 
 
 REACH = 2
-
-
-def shifted(array, axis, by):
-    size = lax.axis_size(axis)
-    pairs = [(i, i + by) for i in range(size) if 0 <= i + by < size]
-    return lax.ppermute(array, axis, pairs)
+SPAN = 5
+HEADS = 8
+MESH = pl.DeviceIdType.MESH
+
+
+def places():
+    n, h, size = lax.axis_index("node"), lax.axis_index("head"), lax.axis_size("node")
+    return n, h, lax.rem(n + 1, size), lax.rem(n + size - 1, size)
+
+
+def greet(n, h, up, down):
+    barrier = pltpu.get_barrier_semaphore()
+    for r in range(1, HEADS):
+        pl.semaphore_signal(barrier, inc=1, device_id=(n, lax.rem(h + r, HEADS)), device_id_type=MESH)
+    for other in (up, down):
+        pl.semaphore_signal(barrier, inc=1, device_id=(other, h), device_id_type=MESH)
+    pl.semaphore_wait(barrier, HEADS + 1)
+
+
+def send(src, dst, ssem, rsem, device):
+    return pltpu.make_async_remote_copy(src_ref=src, dst_ref=dst, send_sem=ssem, recv_sem=rsem, device_id=device, device_id_type=MESH)
+
+
+def columns(c):
+    return pl.ds(pl.multiple_of(c * CL, CL), CL)
+
+
+def fetch_kernel(k, v, q, g, nk, nv, oq, og, lsem, asend, arecv, fsend, frecv):
+    n, h, up, down = places()
+    sources = (k, v, q, g)
+    own = (nk.at[REACH], nv.at[REACH], oq, og)
+    near = (nk, nv)
+
+    def local(a):
+        return pltpu.make_async_copy(sources[a].at[:, columns(h)], own[a].at[h], lsem.at[a])
+
+    def across(a, r):
+        to = lax.rem(h + r, HEADS)
+        return send(sources[a].at[:, columns(to)], own[a].at[h], asend.at[a, r], arecv.at[a, r], (n, to))
+
+    def step(a, way, r):
+        c = lax.rem(h + HEADS - r, HEADS)
+        start, end = ((2, 1), (2, 3), (1, 0), (3, 4))[way]
+        return send(near[a].at[start, c], near[a].at[end, c], fsend.at[a, way, r], frecv.at[a, way, r], (down if way % 2 else up, h))
+
+    for a in range(4):
+        local(a).start()
+    greet(n, h, up, down)
+
+    def loop(first, body):
+        def run(r, carry):
+            body(r)
+            return carry
+        lax.fori_loop(first, HEADS, run, 0)
+
+    for a in range(4):
+        loop(1, lambda r: across(a, r).start())
+    for a in range(2):
+        local(a).wait()
+        step(a, 0, 0).start()
+        step(a, 1, 0).start()
+
+        def on(r):
+            across(a, r).wait_recv()
+            step(a, 0, r).start()
+            step(a, 1, r).start()
+        loop(1, on)
+    for a in range(2):
+        def relay(r):
+            step(a, 0, r).wait_recv()
+            step(a, 2, r).start()
+            step(a, 1, r).wait_recv()
+            step(a, 3, r).start()
+        loop(0, relay)
+    for a in range(2, 4):
+        local(a).wait()
+        loop(1, lambda r: across(a, r).wait_recv())
+    for a in range(4):
+        loop(1, lambda r: across(a, r).wait_send())
+    for a in range(2):
+        def last(r):
+            step(a, 2, r).wait_recv()
+            step(a, 3, r).wait_recv()
+            for way in range(4):
+                step(a, way, r).wait_send()
+        loop(0, last)
+
+
+def fetch(k, v, q, g):
+    bf = jnp.bfloat16
+    anywhere = pl.BlockSpec(memory_space=pl.ANY)
+    near = jax.ShapeDtypeStruct((SPAN, HEADS, CL, CL), bf)
+    own = jax.ShapeDtypeStruct((HEADS, CL, CL), bf)
+    dma = pltpu.SemaphoreType.DMA
+    return pl.pallas_call(
+        fetch_kernel,
+        out_shape=(near, near, own, own),
+        in_specs=[anywhere] * 4,
+        out_specs=(anywhere,) * 4,
+        scratch_shapes=[dma((4,)), dma((4, HEADS)), dma((4, HEADS)), dma((2, 4, HEADS)), dma((2, 4, HEADS))],
+        compiler_params=pltpu.CompilerParams(collective_id=0, has_side_effects=True),
+    )(k, v, q, g)
+
+
+def give_kernel(gk, gv, gq, ok, ov, oq, came, left, total, lsem, asend, arecv, fsend, frecv):
+    n, h, up, down = places()
+    parts = (gk, gv)
+    outs = (ok, ov, oq)
+
+    def final(a, c):
+        return gq.at[c] if a == 2 else total.at[a, c]
+
+    def local(a):
+        return pltpu.make_async_copy(final(a, h), outs[a].at[:, columns(h)], lsem.at[a])
+
+    def across(a, r):
+        to = lax.rem(h + r, HEADS)
+        return send(final(a, to), outs[a].at[:, columns(h)], asend.at[a, r], arecv.at[a, r], (n, to))
+
+    def step(a, way, r):
+        c = lax.rem(h + r, HEADS)
+        src = (parts[a].at[4, c], parts[a].at[0, c], left.at[a, 0, c], left.at[a, 1, c])[way]
+        return send(src, came.at[a, way, c], fsend.at[a, way, r], frecv.at[a, way, r], (down if way % 2 else up, h))
+
+    def loop(first, body):
+        def run(r, carry):
+            body(r)
+            return carry
+        lax.fori_loop(first, HEADS, run, 0)
+
+    def add(*terms):
+        acc = terms[0].astype(jnp.float32)
+        for t in terms[1:]:
+            acc = acc + t.astype(jnp.float32)
+        return acc.astype(jnp.bfloat16)
+
+    greet(n, h, up, down)
+    local(2).start()
+    for a in range(2):
+        def out(r):
+            step(a, 0, r).start()
+            step(a, 1, r).start()
+        loop(0, out)
+    loop(1, lambda r: across(2, r).start())
+    for a in range(2):
+        def relay(r):
+            c = lax.rem(h + r, HEADS)
+            step(a, 0, r).wait_recv()
+            left[a, 0, c] = add(parts[a][3, c], came[a, 0, c])
+            step(a, 2, r).start()
+            step(a, 1, r).wait_recv()
+            left[a, 1, c] = add(parts[a][1, c], came[a, 1, c])
+            step(a, 3, r).start()
+        loop(0, relay)
+    for a in range(2):
+        def finish(r):
+            c = lax.rem(h + r, HEADS)
+            step(a, 2, r).wait_recv()
+            step(a, 3, r).wait_recv()
+            total[a, c] = add(parts[a][2, c], came[a, 2, c], came[a, 3, c])
+        finish(0)
+        local(a).start()
+
+        def rest(r):
+            finish(r)
+            across(a, r).start()
+        loop(1, rest)
+    for a in range(3):
+        local(a).wait()
+
+        def end(r):
+            across(a, r).wait_recv()
+            across(a, r).wait_send()
+        loop(1, end)
+    for a in range(2):
+        def sent(r):
+            for way in range(4):
+                step(a, way, r).wait_send()
+        loop(0, sent)
+
+
+def give(gk, gv, gq):
+    bf = jnp.bfloat16
+    anywhere = pl.BlockSpec(memory_space=pl.ANY)
+    inside = pl.BlockSpec(memory_space=pltpu.VMEM)
+    out = jax.ShapeDtypeStruct((CL, HEADS * CL), bf)
+    dma = pltpu.SemaphoreType.DMA
+    return pl.pallas_call(
+        give_kernel,
+        out_shape=(out, out, out),
+        in_specs=[inside] * 3,
+        out_specs=(anywhere,) * 3,
+        scratch_shapes=[pltpu.VMEM((2, 4, HEADS, CL, CL), bf), pltpu.VMEM((2, 2, HEADS, CL, CL), bf), pltpu.VMEM((2, HEADS, CL, CL), bf), dma((3,)), dma((3, HEADS)), dma((3, HEADS)), dma((2, 4, HEADS)), dma((2, 4, HEADS))],
+        compiler_params=pltpu.CompilerParams(collective_id=1, has_side_effects=True),
+    )(gk, gv, gq)
 
 
 def on_device(query_rows, key_rows, value_rows, grad_out, heat_bias, block_pattern):
-    def enter(a):
-        return lax.all_to_all(a, "head", split_axis=1, concat_axis=0, tiled=True).reshape(CPN, CL, CL)
-
-    def leave(a):
-        return lax.all_to_all(a.reshape(CPN * CL, CL), "head", split_axis=0, concat_axis=1, tiled=True)
-
-    k, v, q, g = enter(key_rows), enter(value_rows), enter(query_rows), enter(grad_out)
+    near_k, near_v, q, g = fetch(key_rows, value_rows, query_rows, grad_out)
     shard = lax.axis_index("node")
-    offsets = list(range(-REACH, REACH + 1))
-    near_k = jnp.concatenate([k if o == 0 else shifted(k, "node", -o) for o in offsets], axis=0)
-    near_v = jnp.concatenate([v if o == 0 else shifted(v, "node", -o) for o in offsets], axis=0)
     index = jnp.where(block_pattern < 0, -1, block_pattern - (shard - REACH) * CPN).reshape(-1)
-    gq, gk, gv = attend(index, q, g, heat_bias, near_k, near_v)
-
-    def total(parts):
-        acc = parts[REACH * CPN : (REACH + 1) * CPN].astype(jnp.float32)
-        for o in offsets:
-            if o != 0:
-                first = (o + REACH) * CPN
-                acc = acc + shifted(parts[first : first + CPN], "node", o).astype(jnp.float32)
-        return acc.astype(jnp.bfloat16)
-
-    return leave(gq), leave(total(gk)), leave(total(gv))
+    shape = (SPAN * HEADS, CL, CL)
+    gq, gk, gv = attend(index, q, g, heat_bias, near_k.reshape(shape), near_v.reshape(shape))
+    shape = (SPAN, HEADS, CL, CL)
+    grad_key, grad_value, grad_query = give(gk.reshape(shape), gv.reshape(shape), gq)
+    return grad_query, grad_key, grad_value
 
 
 def solution(mesh):

time: 177 us -> 110 us (0.62)
  the two profiles are of different devices: /device:TPU:128 before, /device:TPU:1 now
where the time goes in v2:
time: 110 us
  Pallas kernels  103 us (94%)
  local copies, waits for them, and re-layouts  5.6 us (5%)
    pallas_call x1, Pallas kernels, fetch(): pl.pallas_call(fetch_kernel, out_shape=(near, near, own, own), in_specs=[...  40.8 us
    pallas_call x1, Pallas kernels, give(): pl.pallas_call(give_kernel, out_shape=(out, out, out), in_specs=[inside]...  35.4 us
    pallas_call x1, Pallas kernels, attend(): pl.pallas_call(functools.partial(attend_kernel, CH=CH), out_shape=(jax.Sh...  26.4 us
    unnamed x3, local copies, waits for them, and re-layouts  5.01 us

profile of v2, /device:TPU:1, one launch (start us, length us, event | category | flops | bytes accessed | tf_op | source)
XLA Modules:
  0.0 109.6 jit_solution(17845605525259845504)
XLA Ops:
  0.6 0.7 subtract_select_fusion
  1.3 0.6 reshape.21.idx_ref
  1.9 40.8 %shard_map.85 = (bf16[5,8,128,128]{3,2,1,0:T(8,128)(2,1)}, bf16[5,8,128,128]{3,2,1,0:T(8,128)(2,1)}, bf16[8,128,128]{2,1,0:T(8,128)(2,1)}, bf16[8,128,128]{2,1,0:T(8,128)(2,1)}) custom-call(bf16[128,1024]{1,0:T(8,128)(2,1)} %k.1, bf16[128,1024]{1,0:T(8,128)(2,1)} %v.1, bf16[128,1024]{1,0:T(8,128)(2,1)} %q.1, bf16[128,1024]{1,0:T(8,128)(2,1)} %g.1), custom_call_target="tpu_custom_call" | custom-call | tf_op jit(solution)/shard_map/pallas_call | solution.py:198
  42.7 26.4 %shard_map.86 = (bf16[8,128,128]{2,1,0:T(8,128)(2,1)}, bf16[40,128,128]{2,1,0:T(8,128)(2,1)}, bf16[40,128,128]{2,1,0:T(8,128)(2,1)}) custom-call(s32[128]{0:T(128)} %reshape.21.idx_ref, bf16[8,128,128]{2,1,0:T(8,128)(2,1)} %get-tuple-element.13.q_ref, bf16[8,128,128]{2,1,0:T(8,128)(2,1)} %get-tuple-element.14.g_ref, bf16[8,16,128,128]{3,2,1,0:T(8,128)(2,1)} %b_ref.1, ...), custom_call_target="tpu_custom_call" | custom-call | tf_op jit(solution)/shard_map/pallas_call | solution.py:91
  69.2 35.4 %shard_map.87 = (bf16[128,1024]{1,0:T(8,128)(2,1)}, bf16[128,1024]{1,0:T(8,128)(2,1)}, bf16[128,1024]{1,0:T(8,128)(2,1)}) custom-call(bf16[5,8,128,128]{3,2,1,0:T(8,128)(2,1)} %bitcast.4, bf16[5,8,128,128]{3,2,1,0:T(8,128)(2,1)} %bitcast.5, bf16[8,128,128]{2,1,0:T(8,128)(2,1)} %get-tuple-element.19.gq), custom_call_target="tpu_custom_call" | custom-call | tf_op jit(solution)/shard_map/pallas_call | solution.py:291
  104.6 1.7 %copy.12 = bf16[128,1024]{1,0:T(8,128)(2,1)} copy(bf16[128,1024]{1,0:T(8,128)(2,1)} %get-tuple-element.26) | data formatting | bytes 524288
  106.2 1.7 %copy.13 = bf16[128,1024]{1,0:T(8,128)(2,1)} copy(bf16[128,1024]{1,0:T(8,128)(2,1)} %get-tuple-element.27) | data formatting | bytes 524288
  107.9 1.7 %copy.14 = bf16[128,1024]{1,0:T(8,128)(2,1)} copy(bf16[128,1024]{1,0:T(8,128)(2,1)} %get-tuple-element.28) | data formatting | bytes 524288
